TPU v7x, 32 devices: a whole 2x2x4 slice. The times are simulated.
32 devices in a mesh: groups: 2 (over y), page: 8 (over z, core), head: 2 (over x), sub: 1.
Axes of the slice: x: 2, y: 2, z: 4, core: 2. Of those that a mesh axis runs over, the one named last changes fastest.
Arguments:
- queries: bfloat16 [128, 3, 16384], P(('groups', 'page', 'sub'), None, 'head'), parts along dimension 0, may hold values from -400 to 400
- page_keys: bfloat16 [128, 128, 1024], P(('groups', 'page'), None, 'head'), parts along dimension 0, may hold values from -6 to 6
- page_values: bfloat16 [128, 128, 1024], P(('groups', 'page'), None, 'head'), parts along dimension 0, may hold values from -6 to 6
- page_count: int32 [128], P(('groups', 'page')), parts along dimension 0, may hold values from 1 to 128
- leaf_keys: bfloat16 [128, 128, 1024], P(('groups', 'page', 'sub'), None, 'head'), parts along dimension 0, may hold values from -6 to 6
- leaf_values: bfloat16 [128, 128, 1024], P(('groups', 'page', 'sub'), None, 'head'), parts along dimension 0, may hold values from -6 to 6
- leaf_count: int32 [128], P(('groups', 'page', 'sub')), parts along dimension 0, may hold values from 1 to 128
- new_keys: bfloat16 [128, 3, 1024], P(('groups', 'page', 'sub'), None, 'head'), parts along dimension 0, may hold values from -6 to 6
- new_values: bfloat16 [128, 3, 1024], P(('groups', 'page', 'sub'), None, 'head'), parts along dimension 0, may hold values from -6 to 6
- path_owner: int32 [128, 3], P(('groups', 'page', 'sub')), parts along dimension 0, may hold values from 0 to 7, all different within a row; in each aligned block of 8 rows (0 to 7, 8 to 15, ...) at most 6 rows name the same one
- path_slot: int32 [128, 3], P(('groups', 'page', 'sub')), parts along dimension 0, may hold values from 0 to 7
Outputs:
- attended: bfloat16 [128, 3, 16384], P(('groups', 'page', 'sub'), None, 'head'), parts along dimension 0
There are 2 independent parts, one for each index of `groups`. A program takes and returns all parts, laid end to end along the dimension named above; each array names one. Nothing has to cross between parts.
Inputs may be any that keep to these rules, and one draw needn't show every extreme that they name: `path_owner`: each request names 3 different owners; the requests of one device (aligned blocks of 8 requests) name one owner at most 6 times.
All inputs are finite; a program needn't handle non-finite values.
Results may differ from a plain program's by a relative error of at most 0.0047.
Values may be sent and summed in bfloat16 or wider, within the bound.
A program may use at most 64 MiB of HBM per device.

v0:
```python
import math

import jax
import jax.numpy as jnp
from jax import lax
from jax.sharding import PartitionSpec as P

HD = 128
QH = 128
KVH = 8


def page_states(query_rows, keys, values, counts):
    slot_rows = query_rows.shape[0]
    kv_local = keys.shape[2] // HD
    group_size = QH // KVH
    step_count = query_rows.shape[1] // (kv_local * group_size * HD)
    page_tok = keys.shape[1]
    query_five = query_rows.reshape(slot_rows, step_count, kv_local, group_size, HD)
    key_heads = keys.reshape(slot_rows, page_tok, kv_local, HD)
    value_heads = values.reshape(slot_rows, page_tok, kv_local, HD)
    scores = jnp.einsum(
        "nskgd,ntkd->nskgt", query_five, key_heads, preferred_element_type=jnp.float32
    ) * (1.0 / math.sqrt(HD))
    allowed = jnp.arange(page_tok, dtype=jnp.int32)[None, :] < counts[:, None]
    scores = jnp.where(allowed[:, None, None, None, :], scores, -jnp.inf)
    item_max = jnp.max(scores, axis=-1)
    weights = jnp.exp(scores - item_max[..., None])
    item_total = jnp.sum(weights, axis=-1)
    mixed = jnp.einsum(
        "nskgt,ntkd->nskgd",
        weights.astype(jnp.bfloat16),
        value_heads,
        preferred_element_type=jnp.float32,
    )
    item_out = (mixed / item_total[..., None]).astype(jnp.bfloat16)
    return (
        item_out.reshape(slot_rows, -1),
        item_max.reshape(slot_rows, -1),
        item_total.reshape(slot_rows, -1),
    )


def in_blocks(step_fn, arrays, rows_per_slot):
    owner_count = arrays[0].shape[0]
    slot_width = arrays[0].shape[1]
    wanted_slots = -(-512 // max(1, slot_width * rows_per_slot))
    divisors = [
        candidate
        for candidate in range(1, owner_count + 1)
        if owner_count % candidate == 0 and candidate >= wanted_slots
    ]
    merge_count = min(divisors)
    merged = tuple(
        (
            member.reshape(
                (owner_count // merge_count, merge_count * slot_width) + member.shape[2:]
            )
            for member in arrays
        )
    )
    results = lax.map(step_fn, merged)
    return tuple(
        (member.reshape((owner_count, slot_width) + member.shape[2:]) for member in results)
    )


def shards(
    queries,
    page_keys,
    page_values,
    page_count,
    leaf_keys,
    leaf_values,
    leaf_count,
    new_keys,
    new_values,
    path_owner,
    path_slot,
):
    request_rows, step_count, head_width = queries.shape
    kv_local = page_keys.shape[2] // HD
    group_size = QH // KVH
    page_tok = page_keys.shape[1]
    level_count = path_owner.shape[1]
    owner_count = lax.axis_size("page")
    capacity = max(
        2, min(request_rows, (2 * request_rows * level_count + owner_count - 1) // owner_count)
    )
    score_scale = 1.0 / math.sqrt(HD)
    rows_per_slot = step_count * kv_local * group_size
    item_count = request_rows * level_count
    slot_count = owner_count * capacity
    flat_owner = path_owner.reshape(item_count)
    flat_slot = path_slot.reshape(item_count)
    owner_hot = (flat_owner[:, None] == jnp.arange(owner_count, dtype=jnp.int32)[None, :]).astype(
        jnp.int32
    )
    earlier = jnp.cumsum(owner_hot, axis=0) - owner_hot
    owner_rank = jnp.sum(earlier * owner_hot, axis=1)
    position = flat_owner * capacity + owner_rank
    slot_match = (position[None, :] == jnp.arange(slot_count, dtype=jnp.int32)[:, None]).astype(
        jnp.int32
    )
    item_of_slot = jnp.sum(slot_match * jnp.arange(item_count, dtype=jnp.int32)[None, :], axis=1)
    slot_used = jnp.sum(slot_match, axis=1) > 0
    page_ids = jnp.where(slot_used, jnp.take(flat_slot, item_of_slot, axis=0), 0).reshape(
        owner_count, capacity
    )
    outgoing = jnp.take(queries, item_of_slot // level_count, axis=0).reshape(
        owner_count, capacity, step_count * head_width
    )

    def remote_block(packed):
        block_ids = packed[1]
        return page_states(
            packed[0],
            jnp.take(page_keys, block_ids, axis=0),
            jnp.take(page_values, block_ids, axis=0),
            jnp.take(page_count, block_ids, axis=0),
        )

    states = in_blocks(
        remote_block,
        (
            lax.all_to_all(outgoing, "page", split_axis=0, concat_axis=0, tiled=True),
            lax.all_to_all(page_ids, "page", split_axis=0, concat_axis=0, tiled=True),
        ),
        rows_per_slot,
    )
    out_back = lax.all_to_all(states[0], "page", split_axis=0, concat_axis=0, tiled=True)
    max_back = lax.all_to_all(states[1], "page", split_axis=0, concat_axis=0, tiled=True)
    total_back = lax.all_to_all(states[2], "page", split_axis=0, concat_axis=0, tiled=True)
    item_out = jnp.take(out_back.reshape(slot_count, step_count * head_width), position, axis=0)
    item_out = item_out.astype(jnp.float32).reshape(
        request_rows, level_count, step_count, kv_local, group_size, HD
    )
    item_max = jnp.take(max_back.reshape(slot_count, rows_per_slot), position, axis=0)
    item_max = item_max.reshape(request_rows, level_count, step_count, kv_local, group_size)
    item_total = jnp.take(total_back.reshape(slot_count, rows_per_slot), position, axis=0)
    item_total = item_total.reshape(request_rows, level_count, step_count, kv_local, group_size)
    query_five = queries.reshape(request_rows, step_count, kv_local, group_size, HD)
    leaf_heads = leaf_keys.reshape(request_rows, page_tok, kv_local, HD)
    leaf_value_heads = leaf_values.reshape(request_rows, page_tok, kv_local, HD)
    fresh_heads = new_keys.reshape(request_rows, step_count, kv_local, HD)
    fresh_value_heads = new_values.reshape(request_rows, step_count, kv_local, HD)
    leaf_scores = (
        jnp.einsum("rskgd,rtkd->rskgt", query_five, leaf_heads, preferred_element_type=jnp.float32)
        * score_scale
    )
    leaf_allowed = jnp.arange(page_tok, dtype=jnp.int32)[None, :] < leaf_count[:, None]
    leaf_scores = jnp.where(leaf_allowed[:, None, None, None, :], leaf_scores, -jnp.inf)
    fresh_scores = (
        jnp.einsum("rskgd,rukd->rskgu", query_five, fresh_heads, preferred_element_type=jnp.float32)
        * score_scale
    )
    causal = (
        jnp.arange(step_count, dtype=jnp.int32)[None, :]
        <= jnp.arange(step_count, dtype=jnp.int32)[:, None]
    )
    fresh_scores = jnp.where(causal[None, :, None, None, :], fresh_scores, -jnp.inf)
    local_max = jnp.maximum(jnp.max(leaf_scores, axis=-1), jnp.max(fresh_scores, axis=-1))
    leaf_weights = jnp.exp(leaf_scores - local_max[..., None])
    fresh_weights = jnp.exp(fresh_scores - local_max[..., None])
    local_total = jnp.sum(leaf_weights, axis=-1) + jnp.sum(fresh_weights, axis=-1)
    local_sum = jnp.einsum(
        "rskgt,rtkd->rskgd",
        leaf_weights.astype(jnp.bfloat16),
        leaf_value_heads,
        preferred_element_type=jnp.float32,
    )
    local_sum = local_sum + jnp.einsum(
        "rskgu,rukd->rskgd",
        fresh_weights.astype(jnp.bfloat16),
        fresh_value_heads,
        preferred_element_type=jnp.float32,
    )
    local_out = local_sum / local_total[..., None]
    top_score = jnp.maximum(local_max, jnp.max(item_max, axis=1))
    local_mass = local_total * jnp.exp(local_max - top_score)
    item_mass = item_total * jnp.exp(item_max - top_score[:, None])
    numerator = local_mass[..., None] * local_out + jnp.sum(item_mass[..., None] * item_out, axis=1)
    denominator = local_mass + jnp.sum(item_mass, axis=1)
    return (
        (numerator / denominator[..., None])
        .astype(jnp.bfloat16)
        .reshape(request_rows, step_count, head_width)
    )


def solution(mesh):
    return jax.shard_map(
        shards,
        mesh=mesh,
        in_specs=(
            P(("groups", "page", "sub"), None, "head"),
            P(("groups", "page"), None, "head"),
            P(("groups", "page"), None, "head"),
            P(("groups", "page")),
            P(("groups", "page", "sub"), None, "head"),
            P(("groups", "page", "sub"), None, "head"),
            P(("groups", "page", "sub")),
            P(("groups", "page", "sub"), None, "head"),
            P(("groups", "page", "sub"), None, "head"),
            P(("groups", "page", "sub"), None),
            P(("groups", "page", "sub"), None),
        ),
        out_specs=P(("groups", "page", "sub"), None, "head"),
        check_vma=False,
    )
```

profile of v0, /device:TPU:0, one launch (start us, length us, event | category | flops | bytes accessed | tf_op | source)
XLA Modules:
  0.0 292.9 jit_solution(1077446260876932401)
XLA Ops:
  4.8 6.4 %all-to-all-start = ((s32[8,1,6]{2,1,0:T(1,128)}), s32[8,1,6]{2,1,0:T(1,128)S(1)}, u32[]{:S(2)}, u32[]{:S(2)}) async-start(s32[8,1,6]{2,1,0:T(1,128)} %bitcast.15), calls=%async_computation | async-start | bytes 8192 | tf_op jit(solution)/shard_map/all_to_all | solution.py:127
  11.9 8.4 %gather_fusion.4 = bf16[48,3,8192]{2,0,1:T(8,128)(2,1)S(1)} fusion(bf16[8,3,8192]{2,0,1:T(8,128)(2,1)S(1)} %copy-done, s32[1024]{0:T(1024)S(1)} %get-tuple-element.106), kind=kCustom, calls=%fused_computation.6 | custom fusion | bytes 4718784 | tf_op jit(solution)/shard_map/jit(_take)/gather | solution.py:110
  20.3 3.7 %copy.104 = bf16[48,3,8192]{2,1,0:T(4,128)(2,1)} copy(bf16[48,3,8192]{2,0,1:T(8,128)(2,1)S(1)} %gather_fusion.4) | data formatting | bytes 4718592 | tf_op jit(solution)/shard_map/jit(_take)/gather | solution.py:110
  24.0 6.2 %gather.31 = bf16[8,6,24576]{2,1,0:T(8,128)(2,1)S(1)} reshape(bf16[48,3,8192]{2,1,0:T(4,128)(2,1)} %copy.104) | data formatting | bytes 4718592 | tf_op jit(solution)/shard_map/jit(_take)/gather | solution.py:110
  31.0 2.2 broadcast_select_fusion.3
  33.1 5.2 %all-to-all-start.1 = ((bf16[8,6,24576]{2,1,0:T(8,128)(2,1)}), bf16[8,6,24576]{2,1,0:T(8,128)(2,1)}, u32[]{:S(2)}, u32[]{:S(2)}) async-start(bf16[8,6,24576]{2,1,0:T(8,128)(2,1)} %broadcast_select_fusion.3), calls=%async_computation.1 | async-start | bytes 6291456 | tf_op jit(solution)/shard_map/all_to_all | solution.py:126
  38.4 71.6 %all-to-all-done.1 = bf16[8,6,24576]{2,1,0:T(8,128)(2,1)} async-done(((bf16[8,6,24576]{2,1,0:T(8,128)(2,1)}), bf16[8,6,24576]{2,1,0:T(8,128)(2,1)}, u32[]{:S(2)}, u32[]{:S(2)}) %all-to-all-start.1) | async-done | bytes 2359328 | tf_op jit(solution)/shard_map/all_to_all | solution.py:126
  110.0 77.9 %while.14 = (s32[]{:T(128)}, bf16[8,6,24576]{2,1,0:T(8,128)(2,1)}, f32[8,6,192]{2,1,0:T(8,128)}, f32[8,6,192]{2,1,0:T(8,128)}, s32[8,6]{1,0:T(8,128)S(1)}, /*ind...) while((s32[]{:T(128)}, bf16[8,6,24576]{2,1,0:T(8,128)(2,1)}, ...), condition=%wide.region_11.13_spmd, body=%wide.region_8.12_spmd.sunk | while | flops 77611600 | bytes 16513509 | solution.py:62
  110.7 1.8 gather_fusion.1
  112.5 1.8 gather_fusion.2
  120.4 1.8 gather_fusion.1
  122.2 1.8 gather_fusion.2
  130.1 1.8 gather_fusion.1
  131.9 1.8 gather_fusion.2
  139.8 1.8 gather_fusion.1
  141.7 1.8 gather_fusion.2
  149.6 1.8 gather_fusion.1
  187.8 9.9 %all_to_all.29 = f32[8,6,192]{2,1,0:T(8,128)} all-to-all(f32[8,6,192]{2,1,0:T(8,128)} %get-tuple-element.56), channel_id=1, replica_groups=mesh['groups'=2,'page'=8,'head'=2,'sub'=1] {'page'}, dimensions={0} | all-to-all | bytes 73728 | tf_op jit(solution)/shard_map/all_to_all | solution.py:132
  197.7 9.9 %all_to_all.30 = f32[8,6,192]{2,1,0:T(8,128)} all-to-all(f32[8,6,192]{2,1,0:T(8,128)} %get-tuple-element.57), channel_id=1, replica_groups=mesh['groups'=2,'page'=8,'head'=2,'sub'=1] {'page'}, dimensions={0} | all-to-all | bytes 73728 | tf_op jit(solution)/shard_map/all_to_all | solution.py:133
  207.6 4.6 %all-to-all-start.4 = ((bf16[8,6,24576]{2,1,0:T(8,128)(2,1)}), bf16[8,6,24576]{2,1,0:T(8,128)(2,1)}, u32[]{:S(2)}, u32[]{:S(2)}) async-start(bf16[8,6,24576]{2,1,0:T(8,128)(2,1)} %get-tuple-element.58), calls=%async_computation.4 | async-start | bytes 6291456 | tf_op jit(solution)/shard_map/all_to_all | solution.py:131
  214.4 2.8 fusion.44
  224.6 59.1 %all-to-all-done.4 = bf16[8,6,24576]{2,1,0:T(8,128)(2,1)} async-done(((bf16[8,6,24576]{2,1,0:T(8,128)(2,1)}), bf16[8,6,24576]{2,1,0:T(8,128)(2,1)}, u32[]{:S(2)}, u32[]{:S(2)}) %all-to-all-start.4) | async-done | bytes 2359328 | tf_op jit(solution)/shard_map/all_to_all | solution.py:131
  283.7 2.3 reshape.420
  286.0 2.3 gather_fusion.5
  (275 shorter events, 80.8 us)
Async XLA Ops:
  0.0 11.9 %copy-start = (bf16[8,3,8192]{2,0,1:T(8,128)(2,1)S(1)}, bf16[8,3,8192]{2,0,1:T(8,128)(2,1)}, u32[]{:S(2)}) copy-start(bf16[8,3,8192]{2,0,1:T(8,128)(2,1)} %param.17) | copy-start | bytes 1179652
  1.2 10.7 %copy-start.8 = (s32[24]{0:T(128)}, s32[24]{0:T(128)S(1)}, u32[]{:S(2)}) copy-start(s32[24]{0:T(128)S(1)} %select_reduce_fusion.1) | copy-start | bytes 292
  1.8 0.5 copy-start.11
  4.8 28.3 %all-to-all-start = ((s32[8,1,6]{2,1,0:T(1,128)}), s32[8,1,6]{2,1,0:T(1,128)S(1)}, u32[]{:S(2)}, u32[]{:S(2)}) async-start(s32[8,1,6]{2,1,0:T(1,128)} %bitcast.15), calls=%async_computation | async-start | bytes 8192 | tf_op jit(solution)/shard_map/all_to_all | solution.py:127
  33.1 76.8 %copy-start.1 = (s32[8]{0:T(128)S(1)}, s32[8]{0:T(128)}, u32[]{:S(2)}) copy-start(s32[8]{0:T(128)} %param.20) | copy-start | bytes 100
  33.1 76.8 %all-to-all-start.1 = ((bf16[8,6,24576]{2,1,0:T(8,128)(2,1)}), bf16[8,6,24576]{2,1,0:T(8,128)(2,1)}, u32[]{:S(2)}, u32[]{:S(2)}) async-start(bf16[8,6,24576]{2,1,0:T(8,128)(2,1)} %broadcast_select_fusion.3), calls=%async_computation.1 | async-start | bytes 6291456 | tf_op jit(solution)/shard_map/all_to_all | solution.py:126
  207.6 4.6 %copy-start.9 = (s32[24]{0:T(128)S(1)}, s32[24]{0:T(128)}, u32[]{:S(2)}) copy-start(s32[24]{0:T(128)} %copy-done.8) | copy-start | bytes 292
  207.6 4.7 %copy-start.2 = (bf16[8,128,512]{2,1,0:T(8,128)(2,1)S(1)}, bf16[8,128,512]{2,1,0:T(8,128)(2,1)}, u32[]{:S(2)}) copy-start(bf16[8,128,512]{2,1,0:T(8,128)(2,1)} %param.21) | copy-start | bytes 3145732
  207.6 5.0 %copy-start.3 = (bf16[8,128,512]{2,1,0:T(8,128)(2,1)S(1)}, bf16[8,128,512]{2,1,0:T(8,128)(2,1)}, u32[]{:S(2)}) copy-start(bf16[8,128,512]{2,1,0:T(8,128)(2,1)} %param.22) | copy-start | bytes 3145732
  207.6 76.1 %all-to-all-start.4 = ((bf16[8,6,24576]{2,1,0:T(8,128)(2,1)}), bf16[8,6,24576]{2,1,0:T(8,128)(2,1)}, u32[]{:S(2)}, u32[]{:S(2)}) async-start(bf16[8,6,24576]{2,1,0:T(8,128)(2,1)} %get-tuple-element.58), calls=%async_computation.4 | async-start | bytes 6291456 | tf_op jit(solution)/shard_map/all_to_all | solution.py:131
  212.9 5.8 %copy-start.6 = (f32[8,6,192]{2,1,0:T(8,128)S(1)}, f32[8,6,192]{2,1,0:T(8,128)}, u32[]{:S(2)}) copy-start(f32[8,6,192]{2,1,0:T(8,128)} %all_to_all.29) | copy-start | bytes 110596
  212.9 6.4 %copy-start.5 = (f32[8,6,192]{2,1,0:T(8,128)S(1)}, f32[8,6,192]{2,1,0:T(8,128)}, u32[]{:S(2)}) copy-start(f32[8,6,192]{2,1,0:T(8,128)} %all_to_all.30) | copy-start | bytes 110596
  212.9 7.1 %copy-start.10 = (pred[24]{0:T(512)(128)(4,1)S(1)}, pred[24]{0:T(512)(128)(4,1)}, u32[]{:S(2)}) copy-start(pred[24]{0:T(512)(128)(4,1)} %get-tuple-element.88) | copy-start | bytes 76
  288.3 2.5 copy-start.4
  288.3 2.5 copy-start.7
  288.3 2.5 copy-start.12
where the time goes:
time: 295 us; the launch traced here: 293 us
  waiting for transfers between devices  131 us (44%)
  local copies, waits for them, and re-layouts  93.2 us (32%)
  blocking collectives  19.7 us (7%)
  starting transfers between devices  16.2 us (5%)
  other arithmetic  16 us (5%)
  matrix products  16 us (5%)
    all_to_all x1, waiting for transfers between devices, shards(): lax.all_to_all(outgoing, 'page', split_axis=0, concat_axis=0, tiled=True)  71.6 us
    all_to_all x1, waiting for transfers between devices, shards(): lax.all_to_all(states[0], 'page', split_axis=0, concat_axis=0, tiled=True)  59.1 us
    gather x3, local copies, waits for them, and re-layouts, shards(): jnp.take(queries, item_of_slot // level_count, axis=0)  18.3 us
    gather x8, local copies, waits for them, and re-layouts, remote_block(): jnp.take(page_keys, block_ids, axis=0)  14.6 us
    gather x8, local copies, waits for them, and re-layouts, remote_block(): jnp.take(page_values, block_ids, axis=0)  14.6 us
    dynamic_update_slice x16, local copies, waits for them, and re-layouts, in_blocks(): results = lax.map(step_fn, merged)  11.1 us
    all_to_all x1, blocking collectives, shards(): lax.all_to_all(states[2], 'page', split_axis=0, concat_axis=0, tiled=True)  9.87 us
    all_to_all x1, blocking collectives, shards(): lax.all_to_all(states[1], 'page', split_axis=0, concat_axis=0, tiled=True)  9.87 us
  transfers between devices with their start and end apart: 3, of which 2 were waited for; matrix products, arithmetic and copies ran while one was open for 12% of the time, Pallas kernels for 0%

commit v1 on v0

v1 whole, which is shorter than its diff:
```python
import functools
import math

import jax
import jax.numpy as jnp
from jax import lax
from jax.experimental import pallas as pl
from jax.experimental.pallas import tpu as pltpu
from jax.sharding import PartitionSpec as P

HD = 128
QH = 128
KVH = 8
NEG = -1e30
MESH = pl.DeviceIdType.MESH


def kernel(
    cfg,
    q_ref,
    pk_hbm,
    pv_hbm,
    lk_hbm,
    lv_hbm,
    nk_ref,
    nv_ref,
    meta_hbm,
    out_ref,
    qbuf,
    kbuf,
    vbuf,
    lkbuf,
    lvbuf,
    mbuf,
    msm,
    pout,
    sout,
    pin,
    sin,
    loc_o,
    loc_s,
    q_send,
    q_recv,
    po_send,
    po_recv,
    ps_send,
    ps_recv,
    page_send,
    page_recv,
    page_local,
    leaf_local,
    meta_send,
    meta_recv,
    meta_local,
):
    lanes, nodes, reqs, kv, rows, steps, levels, tok, rp, groups, offset = cfg
    scale = math.log2(math.e) / math.sqrt(HD)
    me = lax.axis_index("page")
    lane = lax.rem(me, lanes)
    z = lax.div(me, lanes)
    zr = nodes - 1 - z
    pieces = reqs // rp
    per_group = pieces // groups

    def dev(node):
        return {"page": node * lanes + lane}

    partner = z * lanes + (lanes - 1 - lane)

    barrier = pltpu.get_barrier_semaphore()
    for k in range(1, nodes):
        pl.semaphore_signal(
            barrier, inc=1, device_id=dev(lax.rem(z + k, nodes)), device_id_type=MESH
        )
    if lanes > 1:
        pl.semaphore_signal(barrier, inc=1, device_id={"page": partner}, device_id_type=MESH)
    pl.semaphore_wait(barrier, nodes - 1 + lanes - 1)

    def q_copy(direction, src_node, i, own):
        rows_at = pl.ds(i * rp, rp)
        to = z + 1 if direction == 0 else z - 1
        src = q_ref.at[rows_at] if own else qbuf.at[src_node, rows_at]
        return pltpu.make_async_remote_copy(
            src_ref=src,
            dst_ref=qbuf.at[src_node, rows_at],
            send_sem=q_send.at[direction, src_node, i],
            recv_sem=q_recv.at[src_node, i],
            device_id=dev(to),
            device_id_type=MESH,
        )

    def p_copies(direction, d, i):
        rows_at = pl.ds(i * rp, rp)
        to = z + 1 if direction == 0 else z - 1
        slot = d if direction == 0 else jnp.where(d == z - 1, nodes, d)
        return (
            pltpu.make_async_remote_copy(
                src_ref=pout.at[d, rows_at],
                dst_ref=pin.at[slot, rows_at],
                send_sem=po_send.at[d, i],
                recv_sem=po_recv.at[slot, i],
                device_id=dev(to),
                device_id_type=MESH,
            ),
            pltpu.make_async_remote_copy(
                src_ref=sout.at[d, rows_at],
                dst_ref=sin.at[slot, rows_at],
                send_sem=ps_send.at[d, i],
                recv_sem=ps_recv.at[slot, i],
                device_id=dev(to),
                device_id_type=MESH,
            ),
        )

    def wait_p(slot, i):
        rows_at = pl.ds(i * rp, rp)
        pltpu.make_async_copy(pin.at[slot, rows_at], pin.at[slot, rows_at], po_recv.at[slot, i]).wait()
        pltpu.make_async_copy(sin.at[slot, rows_at], sin.at[slot, rows_at], ps_recv.at[slot, i]).wait()

    def wait_q(src_node, i):
        rows_at = pl.ds(i * rp, rp)
        pltpu.make_async_copy(
            qbuf.at[src_node, rows_at], qbuf.at[src_node, rows_at], q_recv.at[src_node, i]
        ).wait()

    def meta_copy(k):
        return pltpu.make_async_remote_copy(
            src_ref=meta_hbm,
            dst_ref=mbuf.at[me],
            send_sem=meta_send.at[k],
            recv_sem=meta_recv.at[me],
            device_id=dev(lax.rem(z + k, nodes)) if k < nodes else {"page": partner},
            device_id_type=MESH,
        )

    meta_count = nodes if lanes > 1 else nodes - 1
    for k in range(1, meta_count + 1):
        meta_copy(k).start()

    @pl.loop(0, pieces)
    def _(i):
        @pl.when(z + 1 < nodes)
        def _():
            q_copy(0, z, i, True).start()

        @pl.when(z > 0)
        def _():
            q_copy(1, z, i, True).start()

    def page_copies():
        return (
            pltpu.make_async_remote_copy(
                src_ref=pk_hbm,
                dst_ref=kbuf.at[lane],
                send_sem=page_send.at[0],
                recv_sem=page_recv.at[0],
                device_id={"page": partner},
                device_id_type=MESH,
            ),
            pltpu.make_async_remote_copy(
                src_ref=pv_hbm,
                dst_ref=vbuf.at[lane],
                send_sem=page_send.at[1],
                recv_sem=page_recv.at[1],
                device_id={"page": partner},
                device_id_type=MESH,
            ),
        )

    if lanes > 1:
        for copy in page_copies():
            copy.start()
    local_copies = (
        pltpu.make_async_copy(pk_hbm, kbuf.at[lane], page_local.at[0]),
        pltpu.make_async_copy(pv_hbm, vbuf.at[lane], page_local.at[1]),
        pltpu.make_async_copy(lk_hbm, lkbuf, leaf_local.at[0]),
        pltpu.make_async_copy(lv_hbm, lvbuf, leaf_local.at[1]),
        pltpu.make_async_copy(meta_hbm, msm.at[me], meta_local.at[0]),
    )
    for copy in local_copies:
        copy.start()

    @pl.when(z == 0)
    def _():
        @pl.loop(0, nodes)
        def _(d):
            @pl.loop(0, reqs)
            def _(r):
                pin[d, r] = jnp.zeros((kv * rows, HD), jnp.bfloat16)
                sin[d, r] = jnp.full((8, 128), NEG, jnp.float32)

    @pl.when(zr == 0)
    def _():
        @pl.loop(0, nodes)
        def _(d):
            slot = jnp.where(d == nodes - 1, nodes, d)

            @pl.loop(0, reqs)
            def _(r):
                pin[slot, r] = jnp.zeros((kv * rows, HD), jnp.bfloat16)
                sin[slot, r] = jnp.full((8, 128), NEG, jnp.float32)

    def take_meta(page_at, k):
        pltpu.make_async_copy(mbuf.at[page_at], mbuf.at[page_at], meta_recv.at[page_at]).wait()
        copy = pltpu.make_async_copy(mbuf.at[page_at], msm.at[page_at], meta_local.at[k])
        copy.start()
        return copy

    taken = [
        take_meta(lax.rem(z + k, nodes) * lanes + lane, k) for k in range(1, nodes)
    ]
    if lanes > 1:
        taken.append(take_meta(partner, nodes))
    for copy in taken:
        copy.wait()
    for copy in local_copies:
        copy.wait()
    if lanes > 1:
        for copy in page_copies():
            copy.wait_recv()

    eye = lax.broadcasted_iota(jnp.int32, (rows, 128), 0) == lax.broadcasted_iota(
        jnp.int32, (rows, 128), 1
    )
    token = lax.broadcasted_iota(jnp.int32, (rows, tok), 1)

    def to_column(row):
        return jnp.sum(
            jnp.where(eye, jnp.broadcast_to(row, (rows, 128)), 0.0), axis=1, keepdims=True
        )

    def to_row(column):
        return jnp.sum(
            jnp.where(eye, jnp.broadcast_to(column, (rows, 128)), 0.0), axis=0, keepdims=True
        )

    def scores_of(query, keys):
        return (
            lax.dot_general(
                query, keys, (((1,), (1,)), ((), ())), preferred_element_type=jnp.float32
            )
            * scale
        )

    def page_of(node, r):
        found = []
        for o in range(lanes):
            owner = z * lanes + o
            slot = jnp.int32(0)
            hit = jnp.int32(0)
            for j in range(levels):
                match = msm[node * lanes + lane, r, j] == owner
                slot = jnp.where(match, msm[node * lanes + lane, r, levels + j], slot)
                hit = jnp.where(match, 1, hit)
            found.append((slot, hit * msm[owner, slot, 2 * levels]))
        return found

    def page_scores(query, pages, h):
        cols = pl.ds(h * HD, HD)
        return [
            jnp.where(token < count, scores_of(query, kbuf[o, slot, :, cols]), NEG)
            for o, (slot, count) in enumerate(pages)
        ]

    def attend(parts, values):
        top = functools.reduce(jnp.maximum, [jnp.max(s, axis=1, keepdims=True) for s in parts])
        total = None
        acc = None
        for s, v in zip(parts, values):
            w = jnp.exp2(s - top)
            part_total = jnp.sum(w, axis=1, keepdims=True)
            part = jnp.dot(w.astype(jnp.bfloat16), v, preferred_element_type=jnp.float32)
            total = part_total if total is None else total + part_total
            acc = part if acc is None else acc + part
        return acc, top, total

    def partial(d, r):
        pages = page_of(d, r)
        stats = []
        for h in range(kv):
            cols = pl.ds(h * HD, HD)
            at = pl.ds(h * rows, rows)
            query = qbuf[d, r, at, :]
            acc, top, total = attend(
                page_scores(query, pages, h), [vbuf[o, p[0], :, cols] for o, p in enumerate(pages)]
            )
            came = to_column(sin[d, r, pl.ds(h, 1), :])
            peak = jnp.maximum(top, came)
            a = jnp.exp2(top - peak)
            b = jnp.exp2(came - peak)
            mass = a * total + b
            inv = 1.0 / mass
            pout[d, r, at, :] = (
                acc * (a * inv) + pin[d, r, at, :].astype(jnp.float32) * (b * inv)
            ).astype(jnp.bfloat16)
            stats.append(to_row(peak + jnp.log2(mass)))
        for h in range(kv):
            sout[d, r, pl.ds(h, 1), :] = stats[h]

    new_pad = nk_ref.shape[1]
    new_token = lax.broadcasted_iota(jnp.int32, (rows, new_pad), 1)
    row_step = lax.broadcasted_iota(jnp.int32, (rows, new_pad), 0) // (rows // steps)

    def local(r):
        pages = page_of(z, r)
        leaf_len = msm[me, r, 2 * levels + 1]
        for h in range(kv):
            cols = pl.ds(h * HD, HD)
            at = pl.ds(h * rows, rows)
            query = q_ref[r, at, :]
            parts = page_scores(query, pages, h)
            values = [vbuf[o, p[0], :, cols] for o, p in enumerate(pages)]
            parts.append(jnp.where(token < leaf_len, scores_of(query, lkbuf[r, :, cols]), NEG))
            values.append(lvbuf[r, :, cols])
            parts.append(
                jnp.where(new_token <= row_step, scores_of(query, nk_ref[r, :, cols]), NEG)
            )
            values.append(nv_ref[r, :, cols])
            acc, top, total = attend(parts, values)
            loc_o[r, at, :] = acc * (1.0 / total)
            loc_s[r, pl.ds(h, 1), :] = to_row(top + jnp.log2(total))

    def final(r):
        for h in range(kv):
            at = pl.ds(h * rows, rows)
            own = to_column(loc_s[r, pl.ds(h, 1), :])
            below = to_column(sin[z, r, pl.ds(h, 1), :])
            above = to_column(sin[nodes, r, pl.ds(h, 1), :])
            peak = jnp.maximum(own, jnp.maximum(below, above))
            a = jnp.exp2(own - peak)
            b = jnp.exp2(below - peak)
            c = jnp.exp2(above - peak)
            inv = 1.0 / (a + b + c)
            out_ref[r, at, :] = (
                loc_o[r, at, :] * (a * inv)
                + pin[z, r, at, :].astype(jnp.float32) * (b * inv)
                + pin[nodes, r, at, :].astype(jnp.float32) * (c * inv)
            ).astype(jnp.bfloat16)

    local_step = jnp.where((z == 0) | (zr == 0), nodes, min(2, nodes))

    def piece_work(t, i):
        below = z - t
        above = z + t

        @pl.when(below >= 0)
        def _():
            wait_q(below, i)

            @pl.when(z + 1 < nodes)
            def _():
                q_copy(0, below, i, False).start()

        @pl.when(above < nodes)
        def _():
            wait_q(above, i)

            @pl.when(z > 0)
            def _():
                q_copy(1, above, i, False).start()

        up = t - z

        @pl.when((up > z) & (up < nodes))
        def _():
            @pl.when(z > 0)
            def _():
                wait_p(up, i)

            for j in range(rp):
                partial(up, i * rp + j)
            for copy in p_copies(0, up, i):
                copy.start()

        down = t - zr

        @pl.when((down > zr) & (down < nodes))
        def _():
            d = nodes - 1 - down

            @pl.when(zr > 0)
            def _():
                wait_p(d, i)

            for j in range(rp):
                partial(d, i * rp + j)
            for copy in p_copies(1, d, i):
                copy.start()

        @pl.when(t == local_step)
        def _():
            for j in range(rp):
                local(i * rp + j)

    last = 2 * nodes - 2

    @pl.loop(1, last + 1 + offset * (groups - 1))
    def _(tau):
        for g in range(groups):
            t = tau - offset * g

            @pl.when((t >= 1) & (t <= last))
            def _():
                @pl.loop(g * per_group, (g + 1) * per_group)
                def _(i):
                    piece_work(t, i)

    @pl.loop(0, pieces)
    def _(i):
        @pl.when(z > 0)
        def _():
            wait_p(z, i)

        @pl.when(zr > 0)
        def _():
            wait_p(nodes, i)

        for j in range(rp):
            final(i * rp + j)

    for k in range(1, meta_count + 1):
        meta_copy(k).wait_send()
    if lanes > 1:
        for copy in page_copies():
            copy.wait_send()

    @pl.loop(0, pieces)
    def _(i):
        @pl.when(z + 1 < nodes)
        def _():
            q_copy(0, z, i, True).wait_send()

        @pl.when(z > 0)
        def _():
            q_copy(1, z, i, True).wait_send()

        @pl.loop(0, nodes)
        def _(n):
            @pl.when((n < z) & (z + 1 < nodes))
            def _():
                q_copy(0, n, i, False).wait_send()

            @pl.when((n > z) & (z > 0))
            def _():
                q_copy(1, n, i, False).wait_send()

            @pl.when(n > z)
            def _():
                for copy in p_copies(0, n, i):
                    copy.wait_send()

            @pl.when(n < z)
            def _():
                for copy in p_copies(1, n, i):
                    copy.wait_send()


def shards(
    queries,
    page_keys,
    page_values,
    page_count,
    leaf_keys,
    leaf_values,
    leaf_count,
    new_keys,
    new_values,
    path_owner,
    path_slot,
    lanes,
):
    reqs, steps, head_width = queries.shape
    pages, tok, kv_width = page_keys.shape
    kv = kv_width // HD
    group = QH // KVH
    rows = steps * group
    levels = path_owner.shape[1]
    owners = lax.axis_size("page")
    nodes = owners // lanes
    small = nodes <= 8
    rp = 1 if small else reqs
    groups = GROUPS if small else 1
    offset = nodes
    query_rows = (
        queries.reshape(reqs, steps, kv, group, HD)
        .transpose(0, 2, 1, 3, 4)
        .reshape(reqs, kv * rows, HD)
    )
    new_pad = 16
    pad = ((0, 0), (0, new_pad - steps), (0, 0))
    fresh_keys = jnp.pad(new_keys, pad)
    fresh_values = jnp.pad(new_values, pad)
    meta_rows = max(reqs, pages)
    parts = [path_owner, path_slot, page_count[:, None], leaf_count[:, None]]
    meta = jnp.concatenate(
        [jnp.pad(p, ((0, meta_rows - p.shape[0]), (0, 0))) for p in parts], axis=1
    )
    meta = jnp.pad(meta, ((0, 0), (0, 128 - meta.shape[1])))
    cfg = (lanes, nodes, reqs, kv, rows, steps, levels, tok, rp, groups, offset)
    pieces = reqs // rp
    vmem = pl.BlockSpec(memory_space=pltpu.VMEM)
    hbm = pl.BlockSpec(memory_space=pl.ANY)
    dma = pltpu.SemaphoreType.DMA
    block = (reqs, kv * rows, HD)
    stat = (reqs, 8, 128)
    out = pl.pallas_call(
        functools.partial(kernel, cfg),
        out_shape=jax.ShapeDtypeStruct(block, jnp.bfloat16),
        in_specs=[vmem, hbm, hbm, hbm, hbm, vmem, vmem, hbm],
        out_specs=vmem,
        scratch_shapes=[
            pltpu.VMEM((nodes,) + block, jnp.bfloat16),
            pltpu.VMEM((lanes,) + page_keys.shape, jnp.bfloat16),
            pltpu.VMEM((lanes,) + page_keys.shape, jnp.bfloat16),
            pltpu.VMEM(leaf_keys.shape, jnp.bfloat16),
            pltpu.VMEM(leaf_keys.shape, jnp.bfloat16),
            pltpu.VMEM((owners, meta_rows, 128), jnp.int32),
            pltpu.SMEM((owners, meta_rows, 128), jnp.int32),
            pltpu.VMEM((nodes,) + block, jnp.bfloat16),
            pltpu.VMEM((nodes,) + stat, jnp.float32),
            pltpu.VMEM((nodes + 1,) + block, jnp.bfloat16),
            pltpu.VMEM((nodes + 1,) + stat, jnp.float32),
            pltpu.VMEM(block, jnp.float32),
            pltpu.VMEM(stat, jnp.float32),
            dma((2, nodes, pieces)),
            dma((nodes, pieces)),
            dma((nodes, pieces)),
            dma((nodes + 1, pieces)),
            dma((nodes, pieces)),
            dma((nodes + 1, pieces)),
            dma((2,)),
            dma((2,)),
            dma((2,)),
            dma((2,)),
            dma((nodes + 1,)),
            dma((owners,)),
            dma((nodes + 1,)),
        ],
        compiler_params=pltpu.CompilerParams(
            collective_id=0, has_side_effects=True, vmem_limit_bytes=60 * 1024 * 1024
        ),
    )(
        query_rows,
        page_keys,
        page_values,
        leaf_keys,
        leaf_values,
        fresh_keys,
        fresh_values,
        meta,
    )
    return (
        out.reshape(reqs, kv, steps, group, HD)
        .transpose(0, 2, 1, 3, 4)
        .reshape(reqs, steps, head_width)
    )


GROUPS = 1


def solution(mesh):
    lanes = 2 if mesh.shape["sub"] == 1 and mesh.shape["page"] % 4 == 0 else 1
    return jax.shard_map(
        functools.partial(shards, lanes=lanes),
        mesh=mesh,
        in_specs=(
            P(("groups", "page", "sub"), None, "head"),
            P(("groups", "page"), None, "head"),
            P(("groups", "page"), None, "head"),
            P(("groups", "page")),
            P(("groups", "page", "sub"), None, "head"),
            P(("groups", "page", "sub"), None, "head"),
            P(("groups", "page", "sub")),
            P(("groups", "page", "sub"), None, "head"),
            P(("groups", "page", "sub"), None, "head"),
            P(("groups", "page", "sub"), None),
            P(("groups", "page", "sub"), None),
        ),
        out_specs=P(("groups", "page", "sub"), None, "head"),
        check_vma=False,
    )
```

time: 295 us -> 73.5 us (0.25)
  waiting for transfers between devices: 131 us -> 0 us
  local copies, waits for them, and re-layouts: 93.2 us -> 8.53 us
  Pallas kernels: 0 us -> 64.5 us
  blocking collectives: 19.7 us -> 0 us
  starting transfers between devices: 16.2 us -> 0 us
  matrix products: 16 us -> 0 us
  other arithmetic: 16 us -> 0.08 us
    all_to_all x3 -> x0, waiting for transfers between devices: 131 us -> none  [the longest x1 71.6 us: shards(): lax.all_to_all(outgoing, 'page', split_axis=0, concat_axis=0, tiled=True)]
    pallas_call x0 -> x1, Pallas kernels: none -> 64.5 us  [shards(): pl.pallas_call(functools.partial(kernel, cfg), out_shape=jax.ShapeDtypeSt...]
    gather x32 -> x0, local copies, waits for them, and re-layouts: 57 us -> none  [the longest x3 18.3 us: shards(): jnp.take(queries, item_of_slot // level_count, axis=0)]
    all_to_all x2 -> x0, blocking collectives: 19.7 us -> none  [the longest x1 9.87 us: shards(): lax.all_to_all(states[2], 'page', split_axis=0, concat_axis=0, tiled=True)]
    all_to_all x3 -> x0, starting transfers between devices: 16.2 us -> none  [the longest x1 6.35 us: shards(): lax.all_to_all(page_ids, 'page', split_axis=0, concat_axis=0, tiled=True)]
    dot_general x20 -> x0, matrix products: 16 us -> none  [the longest x8 5.98 us: page_states(): jnp.einsum('nskgd,ntkd->nskgt', query_five, key_heads, preferred_element_...]
    dynamic_update_slice x16 -> x0, local copies, waits for them, and re-layouts: 11.1 us -> none  [in_blocks(): results = lax.map(step_fn, merged)]
    while x16 -> x0, local copies, waits for them, and re-layouts: 8.84 us -> none
  transfers between devices with their start and end apart: 3 -> 0, of which waited for: 2 -> 0; matrix products, arithmetic and copies ran while one was open for 12% -> 0% of each run, Pallas kernels for 0% -> 0%
where the time goes in v1:
time: 73.5 us; the launch traced here: 73.2 us
  Pallas kernels  64.5 us (88%)
  local copies, waits for them, and re-layouts  8.53 us (12%)
    pallas_call x1, Pallas kernels, shards(): pl.pallas_call(functools.partial(kernel, cfg), out_shape=jax.ShapeDtypeSt...  64.5 us
    unnamed x8, local copies, waits for them, and re-layouts  2.29 us
    transpose x1, local copies, waits for them, and re-layouts, shards(): return out.reshape(reqs, kv, steps, group, HD).transpose(0, 2, 1, 3, 4).r...  2 us
    broadcast_in_dim x2, local copies, waits for them, and re-layouts, shards(): parts = [path_owner, path_slot, page_count[:, None], leaf_count[:, None]]  1.51 us

profile of v1, /device:TPU:0, one launch (start us, length us, event | category | flops | bytes accessed | tf_op | source)
XLA Modules:
  0.0 73.2 jit_solution(6229103434086152955)
XLA Ops:
  0.0 0.0 copy-start.1
  0.0 0.0 copy-start
  0.0 0.8 %copy.17 = s32[8,1]{1,0:T(8,128)S(1)} copy(s32[8,1]{0,1:T(1,128)} %bitcast.13) | data formatting | bytes 64 | tf_op jit(solution)/shard_map/broadcast_in_dim | solution.py:494
  0.8 0.7 copy.18
  1.5 0.8 %copy.15 = s32[8,3]{1,0:T(8,128)S(1)} copy(s32[8,3]{0,1:T(4,128)} %param.20) | data formatting | bytes 192 | tf_op args[9]
  2.3 0.8 %copy.16 = s32[8,3]{1,0:T(8,128)S(1)} copy(s32[8,3]{0,1:T(4,128)} %param.21) | data formatting | bytes 192 | tf_op args[10]
  3.0 0.1 pad_add_fusion
  3.1 0.6 pad.13.meta_hbm
  3.7 0.0 copy-done.1
  3.7 0.8 %copy.14 = bf16[8,3,512]{2,1,0:T(4,128)(2,1)S(1)} copy(bf16[8,3,512]{2,0,1:T(8,128)(2,1)} %param.19) | data formatting | bytes 49152 | tf_op args[8]
  4.5 0.7 pad.12.nv_ref
  5.1 0.7 pad.11.nk_ref
  5.8 0.0 copy-done
  5.8 0.8 %copy.12 = bf16[8,3,4,16,128]{4,3,1,2,0:T(8,128)(2,1)} copy(bf16[8,3,4,16,128]{4,0,3,2,1:T(8,128)(2,1)S(1)} %bitcast.12) | data formatting | bytes 786432 | tf_op jit(solution)/shard_map/reshape | solution.py:485
  6.6 64.5 %shard_map.109 = bf16[8,192,128]{2,1,0:T(8,128)(2,1)} custom-call(bf16[8,192,128]{2,1,0:T(8,128)(2,1)} %bitcast.11, bf16[8,128,512]{2,1,0:T(8,128)(2,1)} %pk_hbm.1, bf16[8,128,512]{2,1,0:T(8,128)(2,1)} %pv_hbm.1, bf16[8,128,512]{2,1,0:T(8,128)(2,1)} %lk_hbm.1, bf16[8,128,512]{2,1,0:T(8,128)(2,1)} %lv_hbm.1, bf16[8,16,512]{2,1,0:T(8,128)(2,1)} %pad.11.nk_ref, ...), custom_call_target="tpu_custom_call" | custom-call | tf_op jit(solution)/shard_map/pallas_call | solution.py:506
  71.2 2.0 %copy.19 = bf16[8,3,4,16,128]{4,0,3,2,1:T(8,128)(2,1)} copy(bf16[8,3,4,16,128]{4,3,1,2,0:T(8,128)(2,1)} %bitcast.10) | data formatting | bytes 786432 | tf_op jit(solution)/shard_map/transpose | solution.py:554
  (1 shorter events, 0.0 us)
Async XLA Ops:
  0.0 3.7 %copy-start.1 = (bf16[8,3,512]{2,0,1:T(8,128)(2,1)S(1)}, bf16[8,3,512]{2,0,1:T(8,128)(2,1)}, u32[]{:S(2)}) copy-start(bf16[8,3,512]{2,0,1:T(8,128)(2,1)} %param.18) | copy-start | bytes 73732
  0.0 5.8 %copy-start = (bf16[8,3,8192]{2,0,1:T(8,128)(2,1)S(1)}, bf16[8,3,8192]{2,0,1:T(8,128)(2,1)}, u32[]{:S(2)}) copy-start(bf16[8,3,8192]{2,0,1:T(8,128)(2,1)} %param.11) | copy-start | bytes 1179652

commit v2 on v1

v2 whole, which is shorter than its diff:
```python
import functools
import math

import jax
import jax.numpy as jnp
from jax import lax
from jax.experimental import pallas as pl
from jax.experimental.pallas import tpu as pltpu
from jax.sharding import PartitionSpec as P

HD = 128
QH = 128
KVH = 8
NEG = -1e30
MESH = pl.DeviceIdType.MESH


def kernel(
    cfg,
    q_ref,
    pk_hbm,
    pv_hbm,
    lk_hbm,
    lv_hbm,
    nk_ref,
    nv_ref,
    owner_hbm,
    slot_hbm,
    count_hbm,
    leaf_hbm,
    out_ref,
    qbuf,
    kbuf,
    vbuf,
    lkbuf,
    lvbuf,
    mbuf,
    msm,
    leaf_sm,
    fresh_k,
    fresh_v,
    pout,
    pin,
    loc_o,
    loc_s,
    q_send,
    q_recv,
    po_send,
    po_recv,
    page_send,
    page_recv,
    page_local,
    leaf_local,
    meta_send,
    meta_recv,
    meta_local,
):
    lanes, nodes, reqs, kv, rows, steps, levels, tok, rp, lag, hold, end_local, mid_local = cfg
    scale = math.log2(math.e) / math.sqrt(HD)
    me = lax.axis_index("page")
    lane = lax.rem(me, lanes)
    z = lax.div(me, lanes)
    zr = nodes - 1 - z
    pieces = reqs // rp

    def dev(node):
        return {"page": node * lanes + lane}

    partner = z * lanes + (lanes - 1 - lane)

    barrier = pltpu.get_barrier_semaphore()
    for k in range(1, nodes):
        pl.semaphore_signal(
            barrier, inc=1, device_id=dev(lax.rem(z + k, nodes)), device_id_type=MESH
        )
    if lanes > 1:
        pl.semaphore_signal(barrier, inc=1, device_id={"page": partner}, device_id_type=MESH)
    pl.semaphore_wait(barrier, nodes - 1 + lanes - 1)

    def q_copy(direction, src_node, i, own):
        rows_at = pl.ds(i * rp, rp)
        to = z + 1 if direction == 0 else z - 1
        src = q_ref.at[rows_at] if own else qbuf.at[src_node, rows_at]
        return pltpu.make_async_remote_copy(
            src_ref=src,
            dst_ref=qbuf.at[src_node, rows_at],
            send_sem=q_send.at[direction, src_node, i],
            recv_sem=q_recv.at[src_node, i],
            device_id=dev(to),
            device_id_type=MESH,
        )

    def p_copy(direction, d, i):
        rows_at = pl.ds(i * rp, rp)
        to = z + 1 if direction == 0 else z - 1
        slot = d if direction == 0 else jnp.where(d == z - 1, nodes, d)
        return pltpu.make_async_remote_copy(
            src_ref=pout.at[d, rows_at],
            dst_ref=pin.at[slot, rows_at],
            send_sem=po_send.at[d, i],
            recv_sem=po_recv.at[slot, i],
            device_id=dev(to),
            device_id_type=MESH,
        )

    def wait_p(slot, i):
        rows_at = pl.ds(i * rp, rp)
        pltpu.make_async_copy(pin.at[slot, rows_at], pin.at[slot, rows_at], po_recv.at[slot, i]).wait()

    def wait_q(src_node, i):
        rows_at = pl.ds(i * rp, rp)
        pltpu.make_async_copy(
            qbuf.at[src_node, rows_at], qbuf.at[src_node, rows_at], q_recv.at[src_node, i]
        ).wait()

    def meta_copies(k):
        device = dev(lax.rem(z + k, nodes)) if k < nodes else {"page": partner}
        sources = (owner_hbm, slot_hbm) if k < nodes else (count_hbm,)
        return [
            pltpu.make_async_remote_copy(
                src_ref=src,
                dst_ref=mbuf.at[me, pl.ds(n * 8, src.shape[0])],
                send_sem=meta_send.at[k, n],
                recv_sem=meta_recv.at[me, n],
                device_id=device,
                device_id_type=MESH,
            )
            for n, src in enumerate(sources)
        ]

    meta_count = nodes if lanes > 1 else nodes - 1
    for k in range(1, meta_count + 1):
        for copy in meta_copies(k):
            copy.start()

    def page_copies():
        return (
            pltpu.make_async_remote_copy(
                src_ref=pk_hbm,
                dst_ref=kbuf.at[lane],
                send_sem=page_send.at[0],
                recv_sem=page_recv.at[0],
                device_id={"page": partner},
                device_id_type=MESH,
            ),
            pltpu.make_async_remote_copy(
                src_ref=pv_hbm,
                dst_ref=vbuf.at[lane],
                send_sem=page_send.at[1],
                recv_sem=page_recv.at[1],
                device_id={"page": partner},
                device_id_type=MESH,
            ),
        )

    if lanes > 1:
        for copy in page_copies():
            copy.start()
    local_copies = (
        pltpu.make_async_copy(pk_hbm, kbuf.at[lane], page_local.at[0]),
        pltpu.make_async_copy(pv_hbm, vbuf.at[lane], page_local.at[1]),
        pltpu.make_async_copy(lk_hbm, lkbuf, leaf_local.at[0]),
        pltpu.make_async_copy(lv_hbm, lvbuf, leaf_local.at[1]),
        pltpu.make_async_copy(owner_hbm, msm.at[me, pl.ds(0, levels)], meta_local.at[0, 0]),
        pltpu.make_async_copy(slot_hbm, msm.at[me, pl.ds(8, levels)], meta_local.at[0, 1]),
        pltpu.make_async_copy(count_hbm, msm.at[me, pl.ds(16, 1)], meta_local.at[0, 2]),
        pltpu.make_async_copy(leaf_hbm, leaf_sm, meta_local.at[0, 3]),
    )
    for copy in local_copies:
        copy.start()

    stat_row = lax.broadcasted_iota(jnp.int32, (16, 128), 0)
    empty = jnp.where(stat_row < kv, NEG, 0.0).astype(jnp.bfloat16)
    stat_at = pl.ds(kv * rows, 16)
    fresh_k[...] = jnp.zeros_like(fresh_k)
    fresh_v[...] = jnp.zeros_like(fresh_v)
    for n in range(steps):
        fresh_k[n * reqs : (n + 1) * reqs, :] = nk_ref[n]
        fresh_v[n * reqs : (n + 1) * reqs, :] = nv_ref[n]

    @pl.when(z == 0)
    def _():
        @pl.loop(0, nodes)
        def _(d):
            @pl.loop(0, reqs)
            def _(r):
                pin[d, r] = jnp.zeros((kv * rows + 16, HD), jnp.bfloat16)
                pin[d, r, pl.ds(kv * rows, 16), :] = empty

    @pl.when(zr == 0)
    def _():
        @pl.loop(0, nodes)
        def _(d):
            slot = jnp.where(d == nodes - 1, nodes, d)

            @pl.loop(0, reqs)
            def _(r):
                pin[slot, r] = jnp.zeros((kv * rows + 16, HD), jnp.bfloat16)
                pin[slot, r, pl.ds(kv * rows, 16), :] = empty

    def take_meta(page_at, k, heights, first):
        copies = []
        for n, height in enumerate(heights):
            got = mbuf.at[page_at, pl.ds(n * 8, height)]
            pltpu.make_async_copy(got, got, meta_recv.at[page_at, n]).wait()
            copies.append(
                pltpu.make_async_copy(
                    got, msm.at[page_at, pl.ds(first + n * 8, height)], meta_local.at[k, n]
                )
            )
        for copy in copies:
            copy.start()
        return copies

    def settle():
        taken = []
        for k in range(1, nodes):
            taken += take_meta(lax.rem(z + k, nodes) * lanes + lane, k, (levels, levels), 0)
        if lanes > 1:
            taken += take_meta(partner, nodes, (1,), 16)
        for copy in taken:
            copy.wait()
        for copy in local_copies:
            copy.wait()
        if lanes > 1:
            for copy in page_copies():
                copy.wait_recv()

    eye = lax.broadcasted_iota(jnp.int32, (rows, 128), 0) == lax.broadcasted_iota(
        jnp.int32, (rows, 128), 1
    )
    token = lax.broadcasted_iota(jnp.int32, (rows, tok), 1)

    def to_column(row):
        return jnp.sum(
            jnp.where(eye, jnp.broadcast_to(row, (rows, 128)), 0.0), axis=1, keepdims=True
        )

    def to_row(column):
        return jnp.sum(
            jnp.where(eye, jnp.broadcast_to(column, (rows, 128)), 0.0), axis=0, keepdims=True
        )

    def scores_of(query, keys):
        return (
            lax.dot_general(
                query, keys, (((1,), (1,)), ((), ())), preferred_element_type=jnp.float32
            )
            * scale
        )

    def page_of(node, r):
        found = []
        for o in range(lanes):
            owner = z * lanes + o
            slot = jnp.int32(0)
            hit = jnp.int32(0)
            for j in range(levels):
                match = msm[node * lanes + lane, j, r] == owner
                slot = jnp.where(match, msm[node * lanes + lane, 8 + j, r], slot)
                hit = jnp.where(match, 1, hit)
            found.append((slot, hit * msm[owner, 16, slot]))
        return found

    def page_scores(query, pages, h):
        cols = pl.ds(h * HD, HD)
        return [
            jnp.where(token < count, scores_of(query, kbuf[o, slot, :, cols]), NEG)
            for o, (slot, count) in enumerate(pages)
        ]

    def total_max(parts):
        wide = functools.reduce(jnp.maximum, [s for s in parts if s.shape[1] == tok])
        top = jnp.max(wide, axis=1, keepdims=True)
        for s in parts:
            if s.shape[1] != tok:
                top = jnp.maximum(top, jnp.max(s, axis=1, keepdims=True))
        return top

    def total_sum(parts):
        wide = functools.reduce(jnp.add, [w for w in parts if w.shape[1] == tok])
        total = jnp.sum(wide, axis=1, keepdims=True)
        for w in parts:
            if w.shape[1] != tok:
                total = total + jnp.sum(w, axis=1, keepdims=True)
        return total

    def attend(parts, values):
        heads = range(kv)
        tops = [total_max(parts[h]) for h in heads]
        weights = [[jnp.exp2(s - tops[h]) for s in parts[h]] for h in heads]
        accs = [
            functools.reduce(
                jnp.add,
                [
                    jnp.dot(w.astype(jnp.bfloat16), v, preferred_element_type=jnp.float32)
                    for w, v in zip(weights[h], values[h])
                ],
            )
            for h in heads
        ]
        return accs, tops, [total_sum(weights[h]) for h in heads]

    def stat_rows(packed):
        wide = packed.astype(jnp.float32)
        return [
            wide[h : h + 1] + (wide[kv + h : kv + h + 1] + wide[2 * kv + h : 2 * kv + h + 1])
            for h in range(kv)
        ]

    def pack_stats(columns):
        stat = jnp.zeros((16, 128), jnp.float32)
        for h, column in enumerate(columns):
            stat = jnp.where(lax.rem(stat_row, kv) == h, to_row(column), stat)
        first = stat.astype(jnp.bfloat16).astype(jnp.float32)
        rest = stat - first
        second = rest.astype(jnp.bfloat16).astype(jnp.float32)
        third = rest - second
        return jnp.where(
            stat_row < kv, first, jnp.where(stat_row < 2 * kv, second, third)
        ).astype(jnp.bfloat16)

    def span(h):
        return pl.ds(h * rows, rows)

    def partial(d, r):
        pages = page_of(d, r)
        parts = [page_scores(qbuf[d, r, span(h), :], pages, h) for h in range(kv)]
        values = [
            [vbuf[o, p[0], :, pl.ds(h * HD, HD)] for o, p in enumerate(pages)] for h in range(kv)
        ]
        accs, tops, totals = attend(parts, values)
        came = [to_column(row) for row in stat_rows(pin[d, r, stat_at, :])]
        outs, stats = [], []
        for h in range(kv):
            peak = jnp.maximum(tops[h], came[h])
            a = jnp.exp2(tops[h] - peak)
            b = jnp.exp2(came[h] - peak)
            mass = a * totals[h] + b
            inv = 1.0 / mass
            outs.append(
                accs[h] * (a * inv) + pin[d, r, span(h), :].astype(jnp.float32) * (b * inv)
            )
            stats.append(peak + jnp.log2(mass))
        for h in range(kv):
            pout[d, r, span(h), :] = outs[h].astype(jnp.bfloat16)
        pout[d, r, stat_at, :] = pack_stats(stats)

    new_pad = fresh_k.shape[0]
    new_token = lax.broadcasted_iota(jnp.int32, (rows, new_pad), 1)
    row_step = lax.broadcasted_iota(jnp.int32, (rows, new_pad), 0) // (rows // steps)
    causal = new_token // reqs <= row_step

    def local(r):
        pages = page_of(z, r)
        leaf_len = leaf_sm[0, r]
        fresh = causal & (lax.rem(new_token, reqs) == r)
        parts, values = [], []
        for h in range(kv):
            cols = pl.ds(h * HD, HD)
            query = q_ref[r, span(h), :]
            parts.append(
                page_scores(query, pages, h)
                + [
                    jnp.where(token < leaf_len, scores_of(query, lkbuf[r, :, cols]), NEG),
                    jnp.where(fresh, scores_of(query, fresh_k[:, cols]), NEG),
                ]
            )
            values.append(
                [vbuf[o, p[0], :, cols] for o, p in enumerate(pages)]
                + [lvbuf[r, :, cols], fresh_v[:, cols]]
            )
        accs, tops, totals = attend(parts, values)
        for h in range(kv):
            loc_o[r, span(h), :] = accs[h] * (1.0 / totals[h])
            loc_s[r, pl.ds(h, 1), :] = to_row(tops[h] + jnp.log2(totals[h]))

    def final(r):
        below_rows = stat_rows(pin[z, r, stat_at, :])
        above_rows = stat_rows(pin[nodes, r, stat_at, :])
        outs = []
        for h in range(kv):
            own = to_column(loc_s[r, pl.ds(h, 1), :])
            below = to_column(below_rows[h])
            above = to_column(above_rows[h])
            peak = jnp.maximum(own, jnp.maximum(below, above))
            a = jnp.exp2(own - peak)
            b = jnp.exp2(below - peak)
            c = jnp.exp2(above - peak)
            inv = 1.0 / (a + b + c)
            outs.append(
                loc_o[r, span(h), :] * (a * inv)
                + pin[z, r, span(h), :].astype(jnp.float32) * (b * inv)
                + pin[nodes, r, span(h), :].astype(jnp.float32) * (c * inv)
            )
        for h in range(kv):
            out_ref[r, span(h), :] = outs[h].astype(jnp.bfloat16)

    def chain_place(v, pos, delay):
        index = v - lag * pos - delay
        return index, lax.div(index, pieces), lax.rem(index, pieces)

    def query_work(v, direction):
        pos = z if direction == 0 else zr
        index, s, i = chain_place(v, pos, 0)
        src_node = s if direction == 0 else nodes - 1 - s

        @pl.when((index >= 0) & (s < pos))
        def _():
            wait_q(src_node, i)

            @pl.when(pos < nodes - 1)
            def _():
                q_copy(direction, src_node, i, False).start()

        @pl.when((index >= 0) & (s == pos) & (pos < nodes - 1))
        def _():
            q_copy(direction, z, i, True).start()

    def partial_work(v, direction):
        pos = z if direction == 0 else zr
        index, s, i = chain_place(v, pos, hold)
        ahead = nodes + pos - s
        d = ahead if direction == 0 else nodes - 1 - ahead

        @pl.when((index >= 0) & (s > pos) & (s < nodes) & (pos < nodes - 1))
        def _():
            @pl.when(pos > 0)
            def _():
                wait_p(d, i)

            for j in range(rp):
                partial(d, i * rp + j)
            p_copy(direction, d, i).start()

    at_end = (z == 0) | (zr == 0)
    local_at = jnp.where(at_end, end_local, mid_local)
    settle_at = jnp.minimum(local_at, pieces + hold)

    @pl.loop(0, (nodes + 1) * pieces + lag * (nodes - 1) + hold)
    def _(v):
        for direction in range(2):
            query_work(v, direction)

        @pl.when(v == settle_at)
        def _():
            settle()

        for direction in range(2):
            partial_work(v, direction)

        @pl.when((v >= local_at) & (v < local_at + pieces))
        def _():
            for j in range(rp):
                local((v - local_at) * rp + j)

    @pl.loop(0, pieces)
    def _(i):
        @pl.when(z > 0)
        def _():
            wait_p(z, i)

        @pl.when(zr > 0)
        def _():
            wait_p(nodes, i)

        for j in range(rp):
            final(i * rp + j)

    for k in range(1, meta_count + 1):
        for copy in meta_copies(k):
            copy.wait_send()
    if lanes > 1:
        for copy in page_copies():
            copy.wait_send()

    @pl.loop(0, pieces)
    def _(i):
        @pl.when(z + 1 < nodes)
        def _():
            q_copy(0, z, i, True).wait_send()

        @pl.when(z > 0)
        def _():
            q_copy(1, z, i, True).wait_send()

        @pl.loop(0, nodes)
        def _(n):
            @pl.when((n < z) & (z + 1 < nodes))
            def _():
                q_copy(0, n, i, False).wait_send()

            @pl.when((n > z) & (z > 0))
            def _():
                q_copy(1, n, i, False).wait_send()

            @pl.when(n > z)
            def _():
                p_copy(0, n, i).wait_send()

            @pl.when(n < z)
            def _():
                p_copy(1, n, i).wait_send()


def shards(
    queries,
    page_keys,
    page_values,
    page_count,
    leaf_keys,
    leaf_values,
    leaf_count,
    new_keys,
    new_values,
    path_owner,
    path_slot,
    lanes,
):
    reqs, steps, head_width = queries.shape
    pages, tok, kv_width = page_keys.shape
    kv = kv_width // HD
    group = QH // KVH
    rows = steps * group
    levels = path_owner.shape[1]
    owners = lax.axis_size("page")
    nodes = owners // lanes
    small = nodes <= 8
    rp = 1 if small else reqs
    pieces = reqs // rp
    lag = LAG if small else 1
    hold = max(0, lag * (nodes - 1) - pieces)
    mid_local = pieces
    end_local = END_LOCAL * pieces if small else nodes * pieces
    query_rows = (
        queries.reshape(reqs, steps, kv, group, HD)
        .transpose(0, 2, 1, 3, 4)
        .reshape(reqs, kv * rows, HD)
    )
    assert 3 * kv <= 16 and rows <= 128 and levels <= 8
    cfg = (lanes, nodes, reqs, kv, rows, steps, levels, tok, rp, lag, hold, end_local, mid_local)
    vmem = pl.BlockSpec(memory_space=pltpu.VMEM)
    hbm = pl.BlockSpec(memory_space=pl.ANY)
    dma = pltpu.SemaphoreType.DMA
    block = (reqs, kv * rows, HD)
    stat = (reqs, 8, 128)
    sent = (reqs, kv * rows + 16, HD)
    fresh_rows = -(-steps * reqs // 16) * 16
    out = pl.pallas_call(
        functools.partial(kernel, cfg),
        out_shape=jax.ShapeDtypeStruct(block, jnp.bfloat16),
        in_specs=[vmem, hbm, hbm, hbm, hbm, vmem, vmem, hbm, hbm, hbm, hbm],
        out_specs=vmem,
        scratch_shapes=[
            pltpu.VMEM((nodes,) + block, jnp.bfloat16),
            pltpu.VMEM((lanes,) + page_keys.shape, jnp.bfloat16),
            pltpu.VMEM((lanes,) + page_keys.shape, jnp.bfloat16),
            pltpu.VMEM(leaf_keys.shape, jnp.bfloat16),
            pltpu.VMEM(leaf_keys.shape, jnp.bfloat16),
            pltpu.VMEM((owners, 16, pages), jnp.int32),
            pltpu.SMEM((owners, 24, pages), jnp.int32),
            pltpu.SMEM((1, reqs), jnp.int32),
            pltpu.VMEM((fresh_rows, kv_width), jnp.bfloat16),
            pltpu.VMEM((fresh_rows, kv_width), jnp.bfloat16),
            pltpu.VMEM((nodes,) + sent, jnp.bfloat16),
            pltpu.VMEM((nodes + 1,) + sent, jnp.bfloat16),
            pltpu.VMEM(block, jnp.float32),
            pltpu.VMEM(stat, jnp.float32),
            dma((2, nodes, pieces)),
            dma((nodes, pieces)),
            dma((nodes, pieces)),
            dma((nodes + 1, pieces)),
            dma((2,)),
            dma((2,)),
            dma((2,)),
            dma((2,)),
            dma((nodes + 1, 2)),
            dma((owners, 2)),
            dma((nodes + 1, 4)),
        ],
        compiler_params=pltpu.CompilerParams(
            collective_id=0, has_side_effects=True, vmem_limit_bytes=60 * 1024 * 1024
        ),
    )(
        query_rows,
        page_keys,
        page_values,
        leaf_keys,
        leaf_values,
        new_keys.transpose(1, 0, 2),
        new_values.transpose(1, 0, 2),
        path_owner.T,
        path_slot.T,
        page_count[None, :],
        leaf_count[None, :],
    )
    return (
        out.reshape(reqs, kv, steps, group, HD)
        .transpose(0, 2, 1, 3, 4)
        .reshape(reqs, steps, head_width)
    )


LAG = 3
END_LOCAL = 2


def solution(mesh):
    lanes = 2 if mesh.shape["sub"] == 1 and mesh.shape["page"] % 4 == 0 else 1
    return jax.shard_map(
        functools.partial(shards, lanes=lanes),
        mesh=mesh,
        in_specs=(
            P(("groups", "page", "sub"), None, "head"),
            P(("groups", "page"), None, "head"),
            P(("groups", "page"), None, "head"),
            P(("groups", "page")),
            P(("groups", "page", "sub"), None, "head"),
            P(("groups", "page", "sub"), None, "head"),
            P(("groups", "page", "sub")),
            P(("groups", "page", "sub"), None, "head"),
            P(("groups", "page", "sub"), None, "head"),
            P(("groups", "page", "sub"), None),
            P(("groups", "page", "sub"), None),
        ),
        out_specs=P(("groups", "page", "sub"), None, "head"),
        check_vma=False,
    )
```

time: 73.5 us -> 56.5 us (0.77)
  Pallas kernels: 64.5 us -> 52.5 us
  local copies, waits for them, and re-layouts: 8.53 us -> 3.8 us
    pallas_call x1, Pallas kernels: 64.5 us -> 52.5 us  [shards(): pl.pallas_call(functools.partial(kernel, cfg), out_shape=jax.ShapeDtypeSt...]
    unnamed x8 -> x0, local copies, waits for them, and re-layouts: 2.29 us -> none
    pad x3 -> x0, local copies, waits for them, and re-layouts: 1.91 us -> none  [the longest x1 0.67 us: shards(): fresh_values = jnp.pad(new_values, pad)]
    broadcast_in_dim x2 -> x0, local copies, waits for them, and re-layouts: 1.51 us -> none  [shards(): parts = [path_owner, path_slot, page_count[:, None], leaf_count[:, None]]]
    reshape x1, local copies, waits for them, and re-layouts: 0.81 us -> 1.8 us  [shards(): queries.reshape(reqs, steps, kv, group, HD).transpose(0, 2, 1, 3, 4)]
where the time goes in v2:
time: 56.5 us; the launch traced here: 56.3 us
  Pallas kernels  52.5 us (93%)
  local copies, waits for them, and re-layouts  3.8 us (7%)
    pallas_call x1, Pallas kernels, shards(): pl.pallas_call(functools.partial(kernel, cfg), out_shape=jax.ShapeDtypeSt...  52.5 us
    transpose x1, local copies, waits for them, and re-layouts, shards(): return out.reshape(reqs, kv, steps, group, HD).transpose(0, 2, 1, 3, 4).r...  2 us
    reshape x1, local copies, waits for them, and re-layouts, shards(): queries.reshape(reqs, steps, kv, group, HD).transpose(0, 2, 1, 3, 4)  1.8 us

profile of v2, /device:TPU:0, one launch (start us, length us, event | category | flops | bytes accessed | tf_op | source)
XLA Modules:
  0.0 56.3 jit_solution(14003902830718489358)
XLA Ops:
  0.0 1.8 %copy.12 = bf16[8,3,4,16,128]{4,3,1,2,0:T(8,128)(2,1)} copy(bf16[8,3,4,16,128]{4,0,3,2,1:T(8,128)(2,1)} %bitcast.16) | data formatting | bytes 786432 | tf_op jit(solution)/shard_map/reshape | solution.py:536
  1.8 52.5 %shard_map.109 = bf16[8,192,128]{2,1,0:T(8,128)(2,1)} custom-call(bf16[8,192,128]{2,1,0:T(8,128)(2,1)} %bitcast.15, bf16[8,128,512]{2,1,0:T(8,128)(2,1)} %pk_hbm.1, bf16[8,128,512]{2,1,0:T(8,128)(2,1)} %pv_hbm.1, bf16[8,128,512]{2,1,0:T(8,128)(2,1)} %lk_hbm.1, bf16[8,128,512]{2,1,0:T(8,128)(2,1)} %lv_hbm.1, bf16[3,8,512]{2,1,0:T(8,128)(2,1)} %bitcast.17, ...), custom_call_target="tpu_custom_call" | custom-call | tf_op jit(solution)/shard_map/pallas_call | solution.py:549
  54.3 2.0 %copy.13 = bf16[8,3,4,16,128]{4,0,3,2,1:T(8,128)(2,1)} copy(bf16[8,3,4,16,128]{4,3,1,2,0:T(8,128)(2,1)} %bitcast.14) | data formatting | bytes 786432 | tf_op jit(solution)/shard_map/transpose | solution.py:599

commit v3 on v2

--- a/solution.py
+++ b/solution.py
@@ -68,6 +68,19 @@
 
     partner = z * lanes + (lanes - 1 - lane)
 
+    local_copies = (
+        pltpu.make_async_copy(pk_hbm, kbuf.at[lane], page_local.at[0]),
+        pltpu.make_async_copy(pv_hbm, vbuf.at[lane], page_local.at[1]),
+        pltpu.make_async_copy(lk_hbm, lkbuf, leaf_local.at[0]),
+        pltpu.make_async_copy(lv_hbm, lvbuf, leaf_local.at[1]),
+        pltpu.make_async_copy(owner_hbm, msm.at[me, pl.ds(0, levels)], meta_local.at[0, 0]),
+        pltpu.make_async_copy(slot_hbm, msm.at[me, pl.ds(8, levels)], meta_local.at[0, 1]),
+        pltpu.make_async_copy(count_hbm, msm.at[me, pl.ds(16, 1)], meta_local.at[0, 2]),
+        pltpu.make_async_copy(leaf_hbm, leaf_sm, meta_local.at[0, 3]),
+    )
+    for copy in local_copies:
+        copy.start()
+
     barrier = pltpu.get_barrier_semaphore()
     for k in range(1, nodes):
         pl.semaphore_signal(
@@ -156,19 +169,6 @@
     if lanes > 1:
         for copy in page_copies():
             copy.start()
-    local_copies = (
-        pltpu.make_async_copy(pk_hbm, kbuf.at[lane], page_local.at[0]),
-        pltpu.make_async_copy(pv_hbm, vbuf.at[lane], page_local.at[1]),
-        pltpu.make_async_copy(lk_hbm, lkbuf, leaf_local.at[0]),
-        pltpu.make_async_copy(lv_hbm, lvbuf, leaf_local.at[1]),
-        pltpu.make_async_copy(owner_hbm, msm.at[me, pl.ds(0, levels)], meta_local.at[0, 0]),
-        pltpu.make_async_copy(slot_hbm, msm.at[me, pl.ds(8, levels)], meta_local.at[0, 1]),
-        pltpu.make_async_copy(count_hbm, msm.at[me, pl.ds(16, 1)], meta_local.at[0, 2]),
-        pltpu.make_async_copy(leaf_hbm, leaf_sm, meta_local.at[0, 3]),
-    )
-    for copy in local_copies:
-        copy.start()
-
     stat_row = lax.broadcasted_iota(jnp.int32, (16, 128), 0)
     empty = jnp.where(stat_row < kv, NEG, 0.0).astype(jnp.bfloat16)
     stat_at = pl.ds(kv * rows, 16)
@@ -400,6 +400,9 @@
         index = v - lag * pos - delay
         return index, lax.div(index, pieces), lax.rem(index, pieces)
 
+    def early_of(pos):
+        return jnp.minimum(lag * pos, pieces)
+
     def query_work(v, direction):
         pos = z if direction == 0 else zr
         index, s, i = chain_place(v, pos, 0)
@@ -413,13 +416,13 @@
             def _():
                 q_copy(direction, src_node, i, False).start()
 
-        @pl.when((index >= 0) & (s == pos) & (pos < nodes - 1))
+        @pl.when((index >= 0) & (s == pos) & (i >= early_of(pos)) & (pos < nodes - 1))
         def _():
             q_copy(direction, z, i, True).start()
 
     def partial_work(v, direction):
         pos = z if direction == 0 else zr
-        index, s, i = chain_place(v, pos, hold)
+        index, s, i = chain_place(v, pos, hold - early_of(pos))
         ahead = nodes + pos - s
         d = ahead if direction == 0 else nodes - 1 - ahead
 
@@ -434,10 +437,23 @@
             p_copy(direction, d, i).start()
 
     at_end = (z == 0) | (zr == 0)
+    span_of_loop = max(
+        [(nodes - 1) * pieces + lag * (nodes - 1), end_local + pieces, mid_local + pieces]
+        + [nodes * pieces + lag * n + hold - min(lag * n, pieces) for n in range(nodes - 1)]
+    )
     local_at = jnp.where(at_end, end_local, mid_local)
     settle_at = jnp.minimum(local_at, pieces + hold)
 
-    @pl.loop(0, (nodes + 1) * pieces + lag * (nodes - 1) + hold)
+    for direction in range(2):
+        pos = z if direction == 0 else zr
+
+        @pl.when(pos < nodes - 1)
+        def _():
+            @pl.loop(0, early_of(pos))
+            def _(i):
+                q_copy(direction, z, i, True).start()
+
+    @pl.loop(0, span_of_loop)
     def _(v):
         for direction in range(2):
             query_work(v, direction)
@@ -601,8 +617,8 @@
     )
 
 
-LAG = 3
-END_LOCAL = 2
+LAG = 4
+END_LOCAL = 3
 
 
 def solution(mesh):

time: 56.5 us -> 53.1 us (0.940)
  Pallas kernels: 52.5 us -> 49.1 us
    pallas_call x1, Pallas kernels: 52.5 us -> 49.1 us  [shards(): pl.pallas_call(functools.partial(kernel, cfg), out_shape=jax.ShapeDtypeSt...]
where the time goes in v3:
time: 53.1 us; the launch traced here: 52.9 us
  Pallas kernels  49.1 us (92%)
  local copies, waits for them, and re-layouts  3.8 us (7%)
    pallas_call x1, Pallas kernels, shards(): pl.pallas_call(functools.partial(kernel, cfg), out_shape=jax.ShapeDtypeSt...  49.1 us
    transpose x1, local copies, waits for them, and re-layouts, shards(): return out.reshape(reqs, kv, steps, group, HD).transpose(0, 2, 1, 3, 4).r...  2 us
    reshape x1, local copies, waits for them, and re-layouts, shards(): queries.reshape(reqs, steps, kv, group, HD).transpose(0, 2, 1, 3, 4)  1.8 us

profile of v3, /device:TPU:0, one launch (start us, length us, event | category | flops | bytes accessed | tf_op | source)
XLA Modules:
  0.0 52.9 jit_solution(11767085757040018661)
XLA Ops:
  0.0 1.8 %copy.12 = bf16[8,3,4,16,128]{4,3,1,2,0:T(8,128)(2,1)} copy(bf16[8,3,4,16,128]{4,0,3,2,1:T(8,128)(2,1)} %bitcast.16) | data formatting | bytes 786432 | tf_op jit(solution)/shard_map/reshape | solution.py:552
  1.8 49.1 %shard_map.109 = bf16[8,192,128]{2,1,0:T(8,128)(2,1)} custom-call(bf16[8,192,128]{2,1,0:T(8,128)(2,1)} %bitcast.15, bf16[8,128,512]{2,1,0:T(8,128)(2,1)} %pk_hbm.1, bf16[8,128,512]{2,1,0:T(8,128)(2,1)} %pv_hbm.1, bf16[8,128,512]{2,1,0:T(8,128)(2,1)} %lk_hbm.1, bf16[8,128,512]{2,1,0:T(8,128)(2,1)} %lv_hbm.1, bf16[3,8,512]{2,1,0:T(8,128)(2,1)} %bitcast.17, ...), custom_call_target="tpu_custom_call" | custom-call | tf_op jit(solution)/shard_map/pallas_call | solution.py:565
  50.9 2.0 %copy.13 = bf16[8,3,4,16,128]{4,0,3,2,1:T(8,128)(2,1)} copy(bf16[8,3,4,16,128]{4,3,1,2,0:T(8,128)(2,1)} %bitcast.14) | data formatting | bytes 786432 | tf_op jit(solution)/shard_map/transpose | solution.py:615
